TPU v7x, 32 devices: a whole 2x2x4 slice. The times are simulated.
32 devices in a mesh: row: 8 (over y, x, core), col: 4 (over z).
Axes of the slice: x: 2, y: 2, z: 4, core: 2. Of those that a mesh axis runs over, the one named last changes fastest.
Arguments:
- design: bfloat16 [512, 90112], P(('row', 'col')), may hold values from -6 to 6
- arc_partials: float32 [32, 6, 16], P(('row', 'col')), may hold values from -6 to 6
- arc_id: int32 [32], P(('row', 'col')), may hold values from 0 to 7
- arc_weight: float32 [8], replicated, may hold values from 0.25 to 4
Outputs:
- normal_slab: float32 [90112, 2048], P('row', 'col')
All inputs are finite; a program needn't handle non-finite values.
Results may differ from a plain program's by a relative error of at most 0.0003.
The roundings to bfloat16 on the way count: a program that leaves them out, or rounds other values in their place, can miss the bound.
Values may be sent and summed in bfloat16 or wider, within the bound.
A program may use at most 128 MiB of HBM per device.

v0:
```python
import jax
import jax.numpy as jnp
from jax import lax
from jax.sharding import PartitionSpec as P

SLAB = 2048
ridge = 4.0


def solve_small(matrix, rhs):
    order = matrix.shape[-1]
    for pivot in range(order):
        scale = 1.0 / matrix[..., pivot, pivot]
        row_mat = matrix[..., pivot, :] * scale[..., None]
        row_rhs = rhs[..., pivot, :] * scale[..., None]
        factor = matrix[..., :, pivot]
        matrix = matrix - factor[..., :, None] * row_mat[..., None, :]
        rhs = rhs - factor[..., :, None] * row_rhs[..., None, :]
        matrix = matrix.at[..., pivot, :].set(row_mat)
        rhs = rhs.at[..., pivot, :].set(row_rhs)
    return rhs


def own_reduced(design, arc_partials, arc_id, arc_weight):
    high = lax.Precision.HIGHEST
    slab_rows = design[:, :SLAB].astype(jnp.float32)
    partials = arc_partials[0]
    coupling = jnp.dot(partials, slab_rows, precision=high, preferred_element_type=jnp.float32)
    gram = jnp.dot(partials, partials.T, precision=high, preferred_element_type=jnp.float32)
    arc_count = arc_weight.shape[0]
    select = (jnp.arange(arc_count) == arc_id[0]).astype(jnp.float32)
    arc_gram, arc_coupling = lax.psum(
        (select[:, None, None] * gram[None], select[:, None, None] * coupling[None]), ("row", "col")
    )
    order = partials.shape[0]
    own_gram = jnp.sum(select[:, None, None] * arc_gram, axis=0) + ridge * jnp.eye(
        order, dtype=jnp.float32
    )
    own_coupling = jnp.sum(select[:, None, None] * arc_coupling, axis=0)
    solved = solve_small(own_gram, own_coupling)
    reduced = slab_rows - jnp.dot(
        partials.T, solved, precision=high, preferred_element_type=jnp.float32
    )
    weight = jnp.sum(select * arc_weight)
    return (weight * reduced).astype(jnp.bfloat16)


def make_accumulate(ordered, piece):
    return lax.dot_general(
        piece, ordered, (((0,), (0,)), ((), ())), preferred_element_type=jnp.float32
    )


def col_major(slab_global, row_count, col_count, rows_dev):
    width = slab_global.shape[1]
    ordered = slab_global.reshape(row_count, col_count, rows_dev, width)
    return ordered.transpose(1, 0, 2, 3).reshape(rows_dev * row_count * col_count, width)


def local(design, arc_partials, arc_id, arc_weight):
    rows_dev = design.shape[0]
    row_count = lax.axis_size("row")
    col_count = lax.axis_size("col")
    devices = row_count * col_count
    epochs = rows_dev * devices
    eliminated_own = own_reduced(design, arc_partials, arc_id, arc_weight)
    regrouped = lax.all_to_all(design, "row", split_axis=1, concat_axis=0, tiled=True)
    columns = lax.all_to_all(eliminated_own, "col", split_axis=1, concat_axis=0, tiled=True)
    slab_global = lax.all_gather(columns, "row", axis=0, tiled=True)
    ordered = col_major(slab_global, row_count, col_count, rows_dev)
    normal = make_accumulate(ordered, lax.all_gather(regrouped, "col", axis=0, tiled=True))
    return normal * (1.0 / epochs)


def solution(mesh):
    placed = (P(("row", "col"), None), P(("row", "col"), None, None), P(("row", "col")), P())
    return jax.shard_map(
        local, mesh=mesh, in_specs=placed, out_specs=P("row", "col"), check_vma=False
    )
```

profile of v0, /device:TPU:0, one launch (start us, length us, event | category | flops | bytes accessed | tf_op | source)
XLA Modules:
  0.0 400.1 jit_solution(14108734418693655313)
XLA Ops:
  7.4 3.6 copy.42
  11.0 5.2 %all-to-all-start.1 = ((bf16[16,8,11264]{2,0,1:T(8,128)(2,1)}), bf16[16,8,11264]{2,0,1:T(8,128)(2,1)S(1)}, u32[]{:S(2)}, u32[]{:S(2)}) async-start(bf16[16,8,11264]{2,0,1:T(8,128)(2,1)} %bitcast.64), calls=%async_computation.1 | async-start | bytes 5767168 | tf_op jit(solution)/shard_map/all_to_all | solution.py:67
  16.9 1.0 fusion.3
  17.9 0.8 broadcast_multiply_fusion
  18.8 0.0 all-gather.2.cloned.1.call-start
  18.8 33.2 %all-to-all-done.1 = bf16[16,8,11264]{2,0,1:T(8,128)(2,1)S(1)} async-done(((bf16[16,8,11264]{2,0,1:T(8,128)(2,1)}), bf16[16,8,11264]{2,0,1:T(8,128)(2,1)S(1)}, u32[]{:S(2)}, u32[]{:S(2)}) %all-to-all-start.1) | async-done | bytes 2883616 | tf_op jit(solution)/shard_map/all_to_all | solution.py:67
  52.0 1.6 copy-done
  53.6 0.1 fusion.6
  53.7 0.1 broadcast_multiply_fusion.1
  53.8 50.2 %psum.15 = f32[8,6,6]{2,0,1:T(8,128)S(1)} all-reduce(f32[8,6,6]{2,0,1:T(8,128)S(1)} %broadcast_multiply_fusion.1), channel_id=1, replica_groups=mesh['row'=8,'col'=4] {'row','col'}, use_global_device_ids=true, to_apply=%region_3.0 | all-reduce | flops 288 | bytes 2304 | tf_op jit(solution)/shard_map/psum | solution.py:32
  104.0 0.1 multiply_reduce_fusion.1
  104.1 0.5 slice.240
  105.3 0.1 slice_reduce_fusion.5
  105.4 0.1 multiply_subtract_fusion.10
  105.5 0.6 slice.244
  106.8 0.2 slice_reduce_fusion.4
  107.0 0.1 multiply_subtract_fusion.9
  107.1 0.6 slice.248
  108.4 0.2 slice_reduce_fusion.3
  108.6 0.1 multiply_subtract_fusion.8
  108.7 0.6 slice.252
  110.0 0.2 slice_reduce_fusion.2
  110.2 0.1 multiply_subtract_fusion.7
  110.3 0.6 slice.256
  111.5 0.2 slice_reduce_fusion.1
  111.7 0.1 multiply_subtract_fusion.6
  111.8 0.6 slice.260
  113.2 0.6 fusion.12
  113.8 0.2 slice_reduce_fusion
  114.0 216.3 %all-reduce.2.cloned.1.call-done = f32[8,6,2048]{2,0,1:T(8,128)} async-done(((f32[8,6,2048]{2,0,1:T(8,128)}), f32[8,6,2048]{2,0,1:T(8,128)}) %all-reduce.2.cloned.1.call-update) | async-done | bytes 393232 | tf_op jit(solution)/shard_map/psum | solution.py:32
  330.3 1.2 multiply_reduce_fusion
  331.5 0.1 multiply_subtract_fusion.5
  331.6 0.2 scatter.36
  331.8 0.1 multiply_subtract_fusion.4
  331.9 0.2 scatter.40
  332.1 0.1 multiply_subtract_fusion.3
  332.1 0.2 scatter.44
  332.4 0.1 multiply_subtract_fusion.2
  332.4 0.2 scatter.46
  332.6 0.1 multiply_subtract_fusion.1
  332.7 0.2 scatter.50
  332.9 0.1 multiply_subtract_fusion
  333.0 0.2 scatter.54
  333.2 1.7 fusion.2
  334.9 9.2 %all_to_all.38 = bf16[16,4,512]{2,0,1:T(8,128)(2,1)S(1)} all-to-all(bf16[16,4,512]{2,0,1:T(8,128)(2,1)S(1)} %bitcast.70), channel_id=1, replica_groups=mesh['row'=8,'col'=4] {'col'}, dimensions={1} | all-to-all | bytes 131072 | tf_op jit(solution)/shard_map/all_to_all | solution.py:68
  344.1 9.8 %all_gather.6 = bf16[512,512]{1,0:T(8,128)(2,1)S(1)} all-gather(bf16[64,512]{1,0:T(8,128)(2,1)S(1)} %bitcast.69), channel_id=1, replica_groups=mesh['row'=8,'col'=4] {'row'}, dimensions={0}, use_global_device_ids=true | all-gather | bytes 589824 | tf_op jit(solution)/shard_map/all_gather | solution.py:69
  354.0 15.2 %multiply_bitcast_fusion = f32[11264,512]{0,1:T(8,128)} fusion(bf16[512,512]{1,0:T(8,128)(2,1)S(1)} %bitcast.65, bf16[512,11264]{1,0:T(8,128)(2,1)} %all-gather.2.cloned.1.call-done), kind=kOutput, calls=%fused_computation | convolution fusion | flops 5911347200 | bytes 35127296 | tf_op jit(solution)/shard_map/dot_general | solution.py:49
  369.1 23.5 %copy.24 = f32[11264,512]{1,0:T(8,128)} copy(f32[11264,512]{0,1:T(8,128)} %multiply_bitcast_fusion) | data formatting | bytes 46137344 | tf_op jit(solution)/shard_map/mul | solution.py:72
  (34 shorter events, 0.4 us)
Async XLA Ops:
  7.4 9.5 %copy-start.1 = (f32[1,6,16]{2,0,1:T(1,128)S(1)}, f32[1,6,16]{2,0,1:T(1,128)}, u32[]{:S(2)}) copy-start(f32[1,6,16]{2,0,1:T(1,128)} %param.27) | copy-start | bytes 1156
  7.4 105.8 %copy-start.2 = (f32[8]{0:T(128)S(1)}, f32[8]{0:T(128)}, u32[]{:S(2)}) copy-start(f32[8]{0:T(128)} %param.29) | copy-start | bytes 100
  11.0 41.0 %all-to-all-start.1 = ((bf16[16,8,11264]{2,0,1:T(8,128)(2,1)}), bf16[16,8,11264]{2,0,1:T(8,128)(2,1)S(1)}, u32[]{:S(2)}, u32[]{:S(2)}) async-start(bf16[16,8,11264]{2,0,1:T(8,128)(2,1)} %bitcast.64), calls=%async_computation.1 | async-start | bytes 5767168 | tf_op jit(solution)/shard_map/all_to_all | solution.py:67
  16.2 314.1 %all-reduce.2.cloned.1.call-start = ((), (), s32[]{:S(2)}) async-start(), calls=%async_computation.2 | async-start | bytes 786432 | tf_op jit(solution)/shard_map/psum | solution.py:32
  18.8 335.2 %all-gather.2.cloned.1.call-start = ((), (), s32[]{:S(2)}) async-start(), calls=%async_computation.3 | async-start | bytes 14417920 | tf_op jit(solution)/shard_map/all_gather | solution.py:71
  52.0 1.6 copy-start
Sparse Core Ops, SparseCore 0:
  22.3 307.9 all-reduce.1
Sparse Core Ops, SparseCore 1:
  53.7 201.6 all-gather.1
where the time goes:
time: 401 us; the launch traced here: 400 us
  waiting for transfers between devices  250 us (62%)
  blocking collectives  69.1 us (17%)
  local copies, waits for them, and re-layouts  34.6 us (9%)
  between operations  19.7 us (5%)
  matrix products  18 us (4%)
  starting transfers between devices  5.28 us (1%)
    psum x1, waiting for transfers between devices, own_reduced(): lax.psum((select[:, None, None] * gram[None], select[:, None, None] * cou...  216 us
    psum x1, blocking collectives, own_reduced(): lax.psum((select[:, None, None] * gram[None], select[:, None, None] * cou...  50.2 us
    all_to_all x1, waiting for transfers between devices, local(): lax.all_to_all(design, 'row', split_axis=1, concat_axis=0, tiled=True)  33.2 us
    mul x1, local copies, waits for them, and re-layouts, local(): return normal * (1.0 / epochs)  23.5 us
    dot_general x1, matrix products, make_accumulate(): lax.dot_general(piece, ordered, (((0,), (0,)), ((), ())), preferred_eleme...  15.2 us
    all_gather x1, blocking collectives, local(): slab_global = lax.all_gather(columns, 'row', axis=0, tiled=True)  9.79 us
    all_to_all x1, blocking collectives, local(): lax.all_to_all(eliminated_own, 'col', split_axis=1, concat_axis=0, tiled=...  9.18 us
  transfers between devices with their start and end apart: 3, of which 2 were waited for; matrix products, arithmetic and copies ran while one was open for 3% of the time, Pallas kernels for 0%

commit v1 on v0

--- a/solution.py
+++ b/solution.py
@@ -30,7 +30,10 @@
     arc_count = arc_weight.shape[0]
     select = (jnp.arange(arc_count) == arc_id[0]).astype(jnp.float32)
     arc_gram, arc_coupling = lax.psum(
-        (select[:, None, None] * gram[None], select[:, None, None] * coupling[None]), ("row", "col")
+        lax.psum(
+            (select[:, None, None] * gram[None], select[:, None, None] * coupling[None]), "col"
+        ),
+        "row",
     )
     order = partials.shape[0]
     own_gram = jnp.sum(select[:, None, None] * arc_gram, axis=0) + ridge * jnp.eye(

time: 401 us -> 363 us (0.905)
  waiting for transfers between devices: 250 us -> 223 us
  blocking collectives: 69.1 us -> 59.3 us
    all_gather x1, waiting for transfers between devices: 0.03 us -> 178 us  [local(): lax.all_gather(regrouped, 'col', axis=0, tiled=True)]
    psum x1, waiting for transfers between devices: 216 us -> 39.3 us  [own_reduced(): lax.psum((select[:, None, None] * gram[None], select[:, None, None] * cou...]
    all_to_all x1, waiting for transfers between devices: 33.2 us -> 0.01 us  [local(): lax.all_to_all(design, 'row', split_axis=1, concat_axis=0, tiled=True)]
    psum x1, blocking collectives: 50.2 us -> 17.7 us  [own_reduced(): lax.psum((select[:, None, None] * gram[None], select[:, None, None] * cou...]
    psum x0 -> x1, blocking collectives: none -> 22.4 us  [own_reduced(): lax.psum(lax.psum((select[:, None, None] * gram[None], select[:, None, No...]
    psum x0 -> x1, waiting for transfers between devices: none -> 5.26 us  [own_reduced(): lax.psum(lax.psum((select[:, None, None] * gram[None], select[:, None, No...]
  transfers between devices with their start and end apart: 3 -> 4, of which waited for: 2 -> 3; matrix products, arithmetic and copies ran while one was open for 3% -> 3% of each run, Pallas kernels for 0% -> 0%
where the time goes in v1:
time: 363 us; the launch traced here: 362 us
  waiting for transfers between devices  223 us (61%)
  blocking collectives  59.3 us (16%)
  local copies, waits for them, and re-layouts  34.6 us (10%)
  matrix products  18 us (5%)
  between operations  18 us (5%)
  starting transfers between devices  5.31 us (1%)
  other arithmetic  3.7 us (1%)
    all_gather x1, waiting for transfers between devices, local(): lax.all_gather(regrouped, 'col', axis=0, tiled=True)  178 us
    psum x1, waiting for transfers between devices, own_reduced(): lax.psum((select[:, None, None] * gram[None], select[:, None, None] * cou...  39.3 us
    mul x1, local copies, waits for them, and re-layouts, local(): return normal * (1.0 / epochs)  23.5 us
    psum x1, blocking collectives, own_reduced(): lax.psum(lax.psum((select[:, None, None] * gram[None], select[:, None, No...  22.4 us
    psum x1, blocking collectives, own_reduced(): lax.psum((select[:, None, None] * gram[None], select[:, None, None] * cou...  17.7 us
    dot_general x1, matrix products, make_accumulate(): lax.dot_general(piece, ordered, (((0,), (0,)), ((), ())), preferred_eleme...  15.2 us
    all_to_all x1, blocking collectives, local(): lax.all_to_all(eliminated_own, 'col', split_axis=1, concat_axis=0, tiled=...  10.3 us
    all_gather x1, blocking collectives, local(): slab_global = lax.all_gather(columns, 'row', axis=0, tiled=True)  8.99 us
  transfers between devices with their start and end apart: 4, of which 3 were waited for; matrix products, arithmetic and copies ran while one was open for 3% of the time, Pallas kernels for 0%

profile of v1, /device:TPU:0, one launch (start us, length us, event | category | flops | bytes accessed | tf_op | source)
XLA Modules:
  0.0 361.7 jit_solution(6462691683170628908)
XLA Ops:
  6.5 3.6 copy.42
  10.1 5.2 %all-to-all-start.1 = ((bf16[16,8,11264]{2,0,1:T(8,128)(2,1)}), bf16[16,8,11264]{2,0,1:T(8,128)(2,1)S(1)}, u32[]{:S(2)}, u32[]{:S(2)}) async-start(bf16[16,8,11264]{2,0,1:T(8,128)(2,1)} %bitcast.64), calls=%async_computation.1 | async-start | bytes 5767168 | tf_op jit(solution)/shard_map/all_to_all | solution.py:70
  16.1 1.0 fusion.3
  17.1 0.8 broadcast_multiply_fusion
  18.0 39.3 %all-reduce.3.cloned.1.call-done = f32[8,6,2048]{2,0,1:T(8,128)} async-done(((f32[8,6,2048]{2,0,1:T(8,128)}), f32[8,6,2048]{2,0,1:T(8,128)}) %all-reduce.3.cloned.1.call-update) | async-done | bytes 393232 | tf_op jit(solution)/shard_map/psum | solution.py:33
  57.4 1.6 copy-done
  59.0 0.1 fusion.6
  59.1 0.1 broadcast_multiply_fusion.1
  59.2 17.7 %psum.30 = f32[8,6,6]{2,0,1:T(8,128)S(1)} all-reduce(f32[8,6,6]{2,0,1:T(8,128)S(1)} %broadcast_multiply_fusion.1), channel_id=1, replica_groups=mesh['row'=8,'col'=4] {'col'}, use_global_device_ids=true, to_apply=%region_4.0 | all-reduce | flops 288 | bytes 2304 | tf_op jit(solution)/shard_map/psum | solution.py:33
  76.9 22.4 %psum.31 = f32[8,6,6]{2,0,1:T(8,128)S(1)} all-reduce(f32[8,6,6]{2,0,1:T(8,128)S(1)} %psum.30), channel_id=1, replica_groups=mesh['row'=8,'col'=4] {'row'}, use_global_device_ids=true, to_apply=%region_5.0 | all-reduce | flops 288 | bytes 2304 | tf_op jit(solution)/shard_map/psum | solution.py:32
  99.2 0.1 multiply_reduce_fusion.1
  99.3 0.5 slice.240
  100.6 0.1 slice_reduce_fusion.5
  100.7 0.1 multiply_subtract_fusion.10
  100.8 0.6 slice.244
  102.1 0.2 slice_reduce_fusion.4
  102.3 0.1 multiply_subtract_fusion.9
  102.4 0.6 slice.248
  103.7 0.2 slice_reduce_fusion.3
  103.9 0.1 multiply_subtract_fusion.8
  104.0 0.6 slice.252
  105.3 0.2 slice_reduce_fusion.2
  105.5 0.1 multiply_subtract_fusion.7
  105.6 0.6 slice.256
  106.8 0.2 slice_reduce_fusion.1
  107.1 0.6 slice.260
  108.5 0.6 fusion.12
  109.0 0.2 slice_reduce_fusion
  109.2 5.3 %all-reduce.5.cloned.1.call-done = f32[8,6,2048]{2,0,1:T(8,128)} async-done(((f32[8,6,2048]{2,0,1:T(8,128)}), f32[8,6,2048]{2,0,1:T(8,128)}) %all-reduce.5.cloned.1.call-update) | async-done | bytes 393232 | tf_op jit(solution)/shard_map/psum | solution.py:32
  114.5 1.2 multiply_reduce_fusion
  115.7 0.1 multiply_subtract_fusion.5
  115.8 0.2 scatter.36
  116.0 0.1 multiply_subtract_fusion.4
  116.1 0.2 scatter.40
  116.3 0.1 multiply_subtract_fusion.3
  116.3 0.2 scatter.44
  116.6 0.1 multiply_subtract_fusion.2
  116.6 0.2 scatter.46
  116.8 0.1 multiply_subtract_fusion.1
  116.9 0.2 scatter.50
  117.1 0.1 multiply_subtract_fusion
  117.2 0.2 scatter.54
  117.4 1.7 fusion.2
  119.1 10.3 %all_to_all.38 = bf16[16,4,512]{2,0,1:T(8,128)(2,1)S(1)} all-to-all(bf16[16,4,512]{2,0,1:T(8,128)(2,1)S(1)} %bitcast.70), channel_id=1, replica_groups=mesh['row'=8,'col'=4] {'col'}, dimensions={1} | all-to-all | bytes 131072 | tf_op jit(solution)/shard_map/all_to_all | solution.py:71
  129.4 9.0 %all_gather.6 = bf16[512,512]{1,0:T(8,128)(2,1)S(1)} all-gather(bf16[64,512]{1,0:T(8,128)(2,1)S(1)} %bitcast.69), channel_id=1, replica_groups=mesh['row'=8,'col'=4] {'row'}, dimensions={0}, use_global_device_ids=true | all-gather | bytes 589824 | tf_op jit(solution)/shard_map/all_gather | solution.py:72
  138.4 178.1 %all-gather.2.cloned.1.call-done = bf16[512,11264]{1,0:T(8,128)(2,1)} async-done(((bf16[128,11264]{1,0:T(8,128)(2,1)}), bf16[512,11264]{1,0:T(8,128)(2,1)}) %all-gather.2.cloned.1.call-update) | async-done | bytes 11534352 | tf_op jit(solution)/shard_map/all_gather | solution.py:74
  316.5 15.2 %multiply_bitcast_fusion = f32[11264,512]{0,1:T(8,128)} fusion(bf16[512,512]{1,0:T(8,128)(2,1)S(1)} %bitcast.65, bf16[512,11264]{1,0:T(8,128)(2,1)} %all-gather.2.cloned.1.call-done), kind=kOutput, calls=%fused_computation | convolution fusion | flops 5911347200 | bytes 35127296 | tf_op jit(solution)/shard_map/dot_general | solution.py:52
  331.7 23.5 %copy.24 = f32[11264,512]{1,0:T(8,128)} copy(f32[11264,512]{0,1:T(8,128)} %multiply_bitcast_fusion) | data formatting | bytes 46137344 | tf_op jit(solution)/shard_map/mul | solution.py:75
  (38 shorter events, 0.6 us)
Async XLA Ops:
  6.5 9.5 %copy-start.1 = (f32[1,6,16]{2,0,1:T(1,128)S(1)}, f32[1,6,16]{2,0,1:T(1,128)}, u32[]{:S(2)}) copy-start(f32[1,6,16]{2,0,1:T(1,128)} %param.27) | copy-start | bytes 1156
  6.5 101.9 %copy-start.2 = (f32[8]{0:T(128)S(1)}, f32[8]{0:T(128)}, u32[]{:S(2)}) copy-start(f32[8]{0:T(128)} %param.29) | copy-start | bytes 100
  10.1 47.2 %all-to-all-start.1 = ((bf16[16,8,11264]{2,0,1:T(8,128)(2,1)}), bf16[16,8,11264]{2,0,1:T(8,128)(2,1)S(1)}, u32[]{:S(2)}, u32[]{:S(2)}) async-start(bf16[16,8,11264]{2,0,1:T(8,128)(2,1)} %bitcast.64), calls=%async_computation.1 | async-start | bytes 5767168 | tf_op jit(solution)/shard_map/all_to_all | solution.py:70
  15.3 42.0 %all-reduce.3.cloned.1.call-start = ((), (), s32[]{:S(2)}) async-start(), calls=%async_computation.2 | async-start | bytes 786432 | tf_op jit(solution)/shard_map/psum | solution.py:33
  17.9 96.6 %all-reduce.5.cloned.1.call-start = ((), (), s32[]{:S(2)}) async-start(), calls=%async_computation.3 | async-start | bytes 786432 | tf_op jit(solution)/shard_map/psum | solution.py:32
  57.3 259.2 %all-gather.2.cloned.1.call-start = ((), (), s32[]{:S(2)}) async-start(), calls=%async_computation.4 | async-start | bytes 14417920 | tf_op jit(solution)/shard_map/all_gather | solution.py:74
  57.4 1.6 copy-start
Sparse Core Ops, SparseCore 0:
  18.5 38.7 all-reduce.2
  60.4 54.0 all-reduce.4
  116.1 200.3 all-gather.1
